TPU v7x, 32 devices: a whole 2x2x4 slice. The times are simulated.
32 devices in a mesh: prow: 8 (over z, core), pcol: 4 (over y, x).
Axes of the slice: x: 2, y: 2, z: 4, core: 2. Of those that a mesh axis runs over, the one named last changes fastest.
Arguments:
- diag_block: float32 [256, 256], P('prow', 'pcol'), as said below
- panel: float32 [16384, 256], P('prow', 'pcol'), may hold values from -1.5 to 1.5
- slab: float32 [16384, 1024], P('prow', 'pcol'), may hold values from -6 to 6
Outputs:
- diag_factor: float32 [256, 256], P('prow', 'pcol')
- panel_factor: float32 [16384, 256], P('prow', 'pcol')
- slab_updated: float32 [16384, 1024], P('prow', 'pcol')
Inputs may be any that keep to these rules, and one draw needn't show every extreme that they name: diag_block is symmetric positive definite.
All inputs are finite; a program needn't handle non-finite values.
Results may differ from a plain program's by a relative error of at most 0.0003.
Values sent between devices are 32-bit elements; how exact they have to be, the bound alone decides.
A program may use at most 64 MiB of HBM per device.

v0:
```python
import jax
import jax.numpy as jnp
from jax import lax
from jax.sharding import PartitionSpec as P


def broadcast(block, axis, source):
    block = jnp.where(lax.axis_index(axis) == source, block, jnp.zeros_like(block))
    return lax.psum(block, axis)


def local(diag_block, panel, slab):
    row_count = lax.axis_size("prow")
    col_count = lax.axis_size("pcol")
    row_index = lax.axis_index("prow")
    col_index = lax.axis_index("pcol")
    diag_tile = lax.all_gather(diag_block, "pcol", axis=1, tiled=True)
    full_block = lax.all_gather(diag_tile, "prow", axis=0, tiled=True)
    diag_factor = jnp.linalg.cholesky(full_block)
    block_size = full_block.shape[0]
    col_width = panel.shape[1]
    local_rows = panel.shape[0]
    blocks_here = local_rows // block_size
    group = blocks_here * row_count // col_count
    full_rows = lax.all_gather(panel, "pcol", axis=1, tiled=True)
    inverse = jax.scipy.linalg.solve_triangular(
        diag_factor, jnp.eye(block_size, dtype=jnp.float32), lower=True
    )
    factor = jnp.dot(
        full_rows, inverse.T, precision=lax.Precision.HIGHEST, preferred_element_type=jnp.float32
    )
    diag_out = lax.dynamic_slice(
        diag_factor,
        (row_index * diag_block.shape[0], col_index * diag_block.shape[1]),
        (diag_block.shape[0], diag_block.shape[1]),
    )
    panel_out = lax.dynamic_slice_in_dim(factor, col_index * col_width, col_width, 1)
    target = col_index * group
    root_row = target % row_count
    local_block = target // row_count
    chosen = lax.dynamic_slice_in_dim(factor, local_block * block_size, block_size, 0)
    remote = broadcast(chosen, "prow", root_row)
    product = jnp.dot(
        factor, remote.T, precision=lax.Precision.HIGHEST, preferred_element_type=jnp.float32
    )
    position = jnp.arange(local_rows, dtype=jnp.int32)
    row_global = (
        position // block_size * row_count + row_index
    ) * block_size + position % block_size
    col_global = target * block_size + jnp.arange(block_size, dtype=jnp.int32)
    keep_mask = row_global[:, None] >= col_global[None, :]
    updated = jnp.where(keep_mask, slab - product, slab)
    return (diag_out, panel_out, updated)


def solution(mesh):
    placed = (P("prow", "pcol"), P("prow", "pcol"), P("prow", "pcol"))
    return jax.shard_map(
        local,
        mesh=mesh,
        in_specs=placed,
        out_specs=(P("prow", "pcol"), P("prow", "pcol"), P("prow", "pcol")),
        check_vma=False,
    )
```

profile of v0, /device:TPU:0, one launch (start us, length us, event | category | flops | bytes accessed | tf_op | source)
XLA Modules:
  0.0 166.8 jit_solution(1090098768620998737)
XLA Ops:
  7.2 0.0 all-gather.3.cloned.1.call-start
  7.2 0.7 all-gather.3.cloned.1.call-update
  7.9 0.0 all-reduce.3.cloned.1.call-start
  8.0 9.9 %all-gather = f32[4,64,32]{1,2,0:T(8,128)S(1)} all-gather(f32[1,64,32]{1,2,0:T(8,128)} %bitcast.45), channel_id=1, replica_groups=mesh['prow'=8,'pcol'=4] {'pcol'}, dimensions={0}, use_global_device_ids=true | all-gather | bytes 40960 | tf_op jit(solution)/shard_map/all_gather | solution.py:17
  17.9 0.1 reshape.73
  18.0 14.4 %all_gather.10 = f32[256,256]{1,0:T(8,128)S(1)} all-gather(f32[32,256]{1,0:T(8,128)S(1)} %bitcast.44), channel_id=1, replica_groups=mesh['prow'=8,'pcol'=4] {'prow'}, dimensions={0}, use_global_device_ids=true | all-gather | bytes 294912 | tf_op jit(solution)/shard_map/all_gather | solution.py:18
  32.4 0.1 copy.10
  32.6 11.7 %cholesky.50 = f32[128,128]{1,0:T(8,128)S(1)} custom-call(f32[128,128]{1,0:T(8,128)S(1)} %cholesky.118), custom_call_target="Cholesky" | custom-call | tf_op jit(solution)/shard_map/jit(cholesky)/cholesky | solution.py:19
  44.4 9.8 %custom-call.15 = f32[1,128,128]{1,2,0:T(8,128)S(1)} custom-call(f32[1,128,128]{2,1,0:T(8,128)S(1)} %get-tuple-element.26), custom_call_target="InvertDiagBlocksLowerTriangular" | custom-call | tf_op jit(solution)/shard_map/jit(cholesky)/cholesky | solution.py:19
  54.2 0.2 constant_dynamic-update-slice_fusion
  54.4 0.3 convolution_subtract_fusion.1
  54.7 11.7 %cholesky.105 = f32[128,128]{1,0:T(8,128)S(1)} custom-call(f32[128,128]{1,0:T(8,128)S(1)} %convolution_subtract_fusion.1), custom_call_target="Cholesky" | custom-call | tf_op jit(solution)/shard_map/jit(cholesky)/cholesky | solution.py:19
  66.4 0.6 compare_reduce_fusion
  68.4 0.1 triangular_solve.44
  68.5 4.1 %while.1 = (s32[]{:T(128)}, f32[256,256]{1,0:T(8,128)S(1)}, s32[2,2]{1,0:T(2,128)S(1)}, f32[2,128,128]{2,1,0:T(8,128)S(1)}, s32[]{:T(128)}) while((s32[]{:T(128)}, f32[256,256]{1,0:T(8,128)S(1)}, s32[2,2]{1,0:T(2,128)S(1)}, f32[2,128,128]{2,1,0:T(8,128)S(1)}, s32[]{:T(128)}) %tuple.28), condition=%wide.while_cond, body=%wide.while_body.sunk | while | flops 2 | bytes 131181 | solution.py:26
  68.7 0.6 fusion.34
  69.3 1.4 bitcast_dynamic-update-slice_fusion.2
  70.7 0.6 fusion.34
  71.3 1.4 bitcast_dynamic-update-slice_fusion.2
  72.7 19.7 %custom-call.16 = f32[2,128,128]{1,2,0:T(8,128)S(1)} custom-call(f32[2,128,128]{2,1,0:T(8,128)S(1)} %get-tuple-element.10), custom_call_target="InvertDiagBlocksLowerTriangular" | custom-call | tf_op jit(solution)/shard_map/jit(_solve_triangular)/triangular_solve | solution.py:26
  92.4 0.7 dynamic_slice.9
  93.1 0.3 fusion.6
  93.4 0.3 convolution_subtract_fusion
  93.7 0.3 fusion.9
  94.0 0.0 all-gather.3.cloned.1.call-done
  94.0 3.5 %fusion = f32[256,2048]{1,0:T(8,128)S(1)} fusion(f32[2048,256]{0,1:T(8,128)} %all-gather.3.cloned.1.call-done, f32[128,256]{1,0:T(8,128)S(1)} %fusion.9, f32[128,256]{1,0:T(8,128)S(1)} %fusion.6), kind=kOutput, calls=%fused_computation.6 | convolution fusion | flops 1610678272 | bytes 4456448 | tf_op jit(solution)/shard_map/dot_general | solution.py:29
  97.5 0.7 select_bitcast_fusion
  98.2 0.0 all-reduce.3.cloned.1.call-update
  98.2 0.8 dynamic-slice_bitcast_fusion
  99.1 54.8 %all-reduce.3.cloned.1.call-done = f32[256,256]{0,1:T(8,128)} async-done(((f32[256,256]{0,1:T(8,128)}), f32[256,256]{0,1:T(8,128)}) %all-reduce.3.cloned.1.call-update) | async-done | bytes 262160 | tf_op jit(solution)/shard_map/psum | solution.py:9
  153.9 6.1 %subtract_select_fusion = f32[2048,256]{1,0:T(8,128)} fusion(f32[2048,256]{1,0:T(8,128)} %param.5, f32[256,2048]{1,0:T(8,128)S(1)} %fusion, f32[256,256]{0,1:T(8,128)} %all-reduce.3.cloned.1.call-done, s32[256]{0:T(256)S(1)} %iota_add_fusion, s32[2048]{0:T(1024)S(1)} %fusion.22), kind=kOutput, calls=%fused_computation.2 | convolution fusion | flops 1612185600 | bytes 6562816 | tf_op jit(solution)/shard_map/dot_general | solution.py:43
  (14 shorter events, 0.3 us)
Async XLA Ops:
  7.2 86.8 %all-gather.3.cloned.1.call-start = ((), (), s32[]{:S(2)}) async-start(), calls=%async_computation | async-start | bytes 2621440 | tf_op jit(solution)/shard_map/all_gather | solution.py:25
  7.9 146.0 %all-reduce.3.cloned.1.call-start = ((), (), s32[]{:S(2)}) async-start(), calls=%async_computation.1 | async-start | bytes 524288 | tf_op jit(solution)/shard_map/psum | solution.py:9
Sparse Core Ops, SparseCore 0:
  9.8 37.9 all-gather.2
  98.3 55.4 all-reduce.2
where the time goes:
time: 167 us
  waiting for transfers between devices  55.5 us (33%)
  other arithmetic  54.5 us (33%)
  blocking collectives  24.3 us (15%)
  between operations  15.5 us (9%)
  matrix products  10.9 us (7%)
  local copies, waits for them, and re-layouts  5.85 us (4%)
    psum x1, waiting for transfers between devices, broadcast(): return lax.psum(block, axis)  54.8 us
    another operation x6, other arithmetic, local(): diag_factor = jnp.linalg.cholesky(full_block)  34 us
    another operation x3, other arithmetic, local(): jax.scipy.linalg.solve_triangular(diag_factor, jnp.eye(block_size, dtype=...  19.7 us
    all_gather x1, blocking collectives, local(): full_block = lax.all_gather(diag_tile, 'prow', axis=0, tiled=True)  14.4 us
    all_gather x1, blocking collectives, local(): diag_tile = lax.all_gather(diag_block, 'pcol', axis=1, tiled=True)  9.88 us
    dot_general x1, matrix products, local(): jnp.dot(factor, remote.T, precision=lax.Precision.HIGHEST, preferred_elem...  6.11 us
    another operation x6, local copies, waits for them, and re-layouts  3.95 us
    dot_general x1, matrix products, local(): jnp.dot(full_rows, inverse.T, precision=lax.Precision.HIGHEST, preferred_...  3.47 us
  transfers between devices with their start and end apart: 2, of which 1 were waited for; matrix products, arithmetic and copies ran while one was open for 37% of the time, Pallas kernels for 0%

commit v1 on v0

--- a/solution.py
+++ b/solution.py
@@ -15,7 +15,26 @@
     row_index = lax.axis_index("prow")
     col_index = lax.axis_index("pcol")
     diag_tile = lax.all_gather(diag_block, "pcol", axis=1, tiled=True)
-    full_block = lax.all_gather(diag_tile, "prow", axis=0, tiled=True)
+    size, index, span = (lax.axis_size("prow"), lax.axis_index("prow"), diag_tile.shape[0])
+    ahead = [(i, (i + 1) % size) for i in range(size)]
+    left = [(i, (i - 1) % size) for i in range(size)]
+    whole = jnp.zeros(
+        (*diag_tile.shape[:0], size * span, *diag_tile.shape[0 + 1 :]), diag_tile.dtype
+    )
+    whole = lax.dynamic_update_slice_in_dim(whole, diag_tile, index * span, axis=0)
+    from_left = from_right = diag_tile
+    halfway = size // 2
+    for turn in range(1, halfway + 1):
+        from_left = lax.ppermute(from_left, "prow", ahead)
+        whole = lax.dynamic_update_slice_in_dim(
+            whole, from_left, (index - turn) % size * span, axis=0
+        )
+        if turn < size - halfway:
+            from_right = lax.ppermute(from_right, "prow", left)
+            whole = lax.dynamic_update_slice_in_dim(
+                whole, from_right, (index + turn) % size * span, axis=0
+            )
+    full_block = whole
     diag_factor = jnp.linalg.cholesky(full_block)
     block_size = full_block.shape[0]
     col_width = panel.shape[1]

time: 167 us -> 182 us (1.090)
  blocking collectives: 24.3 us -> 9.88 us
  starting transfers between devices: 0.08 us -> 11.1 us
  local copies, waits for them, and re-layouts: 5.85 us -> 15.1 us
  waiting for transfers between devices: 55.5 us -> 63.9 us
    all_gather x1 -> x0, blocking collectives: 14.4 us -> none  [local(): full_block = lax.all_gather(diag_tile, 'prow', axis=0, tiled=True)]
    ppermute x0 -> x7, starting transfers between devices: none -> 11 us  [the longest x3 10.9 us: local(): from_right = lax.ppermute(from_right, 'prow', left)]
    ppermute x0 -> x7, waiting for transfers between devices: none -> 8.9 us  [the longest x4 8.84 us: local(): from_left = lax.ppermute(from_left, 'prow', ahead)]
    dynamic_update_slice x0 -> x9, local copies, waits for them, and re-layouts: none -> 8.69 us  [the longest x3 4 us: local(): lax.dynamic_update_slice_in_dim(whole, from_right, (index + turn) % size...]
    another operation x6 -> x11, local copies, waits for them, and re-layouts: 3.95 us -> 4.17 us
  transfers between devices with their start and end apart: 2 -> 9, of which waited for: 1 -> 5; matrix products, arithmetic and copies ran while one was open for 37% -> 39% of each run, Pallas kernels for 0% -> 0%
where the time goes in v1:
time: 182 us; the launch traced here: 181 us
  waiting for transfers between devices  63.9 us (35%)
  other arithmetic  54.7 us (30%)
  between operations  15.7 us (9%)
  local copies, waits for them, and re-layouts  15.1 us (8%)
  starting transfers between devices  11.1 us (6%)
  matrix products  10.9 us (6%)
  blocking collectives  9.88 us (5%)
    psum x1, waiting for transfers between devices, broadcast(): return lax.psum(block, axis)  55 us
    another operation x6, other arithmetic, local(): diag_factor = jnp.linalg.cholesky(full_block)  33.9 us
    another operation x3, other arithmetic, local(): jax.scipy.linalg.solve_triangular(diag_factor, jnp.eye(block_size, dtype=...  19.9 us
    ppermute x3, starting transfers between devices, local(): from_right = lax.ppermute(from_right, 'prow', left)  10.9 us
    all_gather x1, blocking collectives, local(): diag_tile = lax.all_gather(diag_block, 'pcol', axis=1, tiled=True)  9.88 us
    ppermute x4, waiting for transfers between devices, local(): from_left = lax.ppermute(from_left, 'prow', ahead)  8.84 us
    dot_general x1, matrix products, local(): jnp.dot(factor, remote.T, precision=lax.Precision.HIGHEST, preferred_elem...  6.1 us
    another operation x11, local copies, waits for them, and re-layouts  4.17 us
  transfers between devices with their start and end apart: 9, of which 5 were waited for; matrix products, arithmetic and copies ran while one was open for 39% of the time, Pallas kernels for 0%

profile of v1, /device:TPU:0, one launch (start us, length us, event | category | flops | bytes accessed | tf_op | source)
XLA Modules:
  0.0 181.3 jit_solution(9311461919702681612)
XLA Ops:
  7.2 9.9 %all-gather = f32[4,64,32]{1,2,0:T(8,128)S(1)} all-gather(f32[1,64,32]{1,2,0:T(8,128)} %bitcast.45), channel_id=1, replica_groups=mesh['prow'=8,'pcol'=4] {'pcol'}, dimensions={0}, use_global_device_ids=true | all-gather | bytes 40960 | tf_op jit(solution)/shard_map/all_gather | solution.py:17
  17.1 0.1 copy.14
  17.2 0.1 collective-permute-start
  17.3 3.5 %collective-permute-start.1 = (f32[32,256]{0,1:T(8,128)S(1)}, f32[32,256]{0,1:T(8,128)S(1)}, u32[]{:S(2)}, u32[]{:S(2)}) collective-permute-start(f32[32,256]{0,1:T(8,128)S(1)} %bitcast.43), channel_id=1, source_target_pairs={{0,28},{4,0},{8,4},{12,8},{16,12},{20,16},{24,20},{28,24},{1,29},{... | collective-permute-start | bytes 98312 | tf_op jit(solution)/shard_map/ppermute | solution.py:33
  20.9 2.6 %collective-permute-done = f32[32,256]{0,1:T(8,128)S(1)} collective-permute-done((f32[32,256]{0,1:T(8,128)S(1)}, f32[32,256]{0,1:T(8,128)S(1)}, u32[]{:S(2)}, u32[]{:S(2)}) %collective-permute-start) | collective-permute-done | bytes 32800 | tf_op jit(solution)/shard_map/ppermute | solution.py:28
  23.6 3.6 %collective-permute-start.3 = (f32[32,256]{0,1:T(8,128)S(1)}, f32[32,256]{0,1:T(8,128)S(1)}, u32[]{:S(2)}, u32[]{:S(2)}) collective-permute-start(f32[32,256]{0,1:T(8,128)S(1)} %collective-permute-done.1), channel_id=1, source_target_pairs={{0,28},{4,0},{8,4},{12,8},{16,12},{20,16},{24,20},{28,24},{1,29},{... | collective-permute-start | bytes 98312 | tf_op jit(solution)/shard_map/ppermute | solution.py:33
  27.1 3.7 %collective-permute-done.2 = f32[32,256]{0,1:T(8,128)S(1)} collective-permute-done((f32[32,256]{0,1:T(8,128)S(1)}, f32[32,256]{0,1:T(8,128)S(1)}, u32[]{:S(2)}, u32[]{:S(2)}) %collective-permute-start.2) | collective-permute-done | bytes 32800 | tf_op jit(solution)/shard_map/ppermute | solution.py:28
  30.9 0.1 collective-permute-done.3
  30.9 3.8 %collective-permute-start.5 = (f32[32,256]{0,1:T(8,128)S(1)}, f32[32,256]{0,1:T(8,128)S(1)}, u32[]{:S(2)}, u32[]{:S(2)}) collective-permute-start(f32[32,256]{0,1:T(8,128)S(1)} %collective-permute-done.3), channel_id=1, source_target_pairs={{0,28},{4,0},{8,4},{12,8},{16,12},{20,16},{24,20},{28,24},{1,29},{... | collective-permute-start | bytes 98312 | tf_op jit(solution)/shard_map/ppermute | solution.py:33
  34.7 2.5 %collective-permute-done.4 = f32[32,256]{0,1:T(8,128)S(1)} collective-permute-done((f32[32,256]{0,1:T(8,128)S(1)}, f32[32,256]{0,1:T(8,128)S(1)}, u32[]{:S(2)}, u32[]{:S(2)}) %collective-permute-start.4) | collective-permute-done | bytes 32800 | tf_op jit(solution)/shard_map/ppermute | solution.py:28
  37.3 1.1 dynamic_update_slice.24
  38.4 0.9 dynamic_update_slice.25
  39.3 1.3 dynamic_update_slice.26
  40.6 0.9 dynamic_update_slice.27
  41.5 1.3 dynamic_update_slice.28
  42.9 0.9 dynamic_update_slice.29
  43.8 1.3 dynamic_update_slice.30
  45.1 0.8 dynamic_update_slice.31
  45.9 0.1 copy.15
  46.1 11.7 %cholesky.49 = f32[128,128]{1,0:T(8,128)S(1)} custom-call(f32[128,128]{1,0:T(8,128)S(1)} %cholesky.115), custom_call_target="Cholesky" | custom-call | tf_op jit(solution)/shard_map/jit(cholesky)/cholesky | solution.py:38
  57.8 0.1 copy.16
  58.0 9.8 %custom-call.15 = f32[1,128,128]{1,2,0:T(8,128)S(1)} custom-call(f32[1,128,128]{2,1,0:T(8,128)S(1)} %get-tuple-element.38), custom_call_target="InvertDiagBlocksLowerTriangular" | custom-call | tf_op jit(solution)/shard_map/jit(cholesky)/cholesky | solution.py:38
  67.8 0.2 fusion.10
  68.0 0.1 copy.17
  68.1 0.3 slice_subtract_fusion
  68.4 11.7 %cholesky.103 = f32[128,128]{1,0:T(8,128)S(1)} custom-call(f32[128,128]{1,0:T(8,128)S(1)} %slice_subtract_fusion), custom_call_target="Cholesky" | custom-call | tf_op jit(solution)/shard_map/jit(cholesky)/cholesky | solution.py:38
  80.1 0.1 copy.18
  80.3 0.6 compare_reduce_fusion
  82.3 0.1 triangular_solve.44
  82.4 4.2 %while.1 = (s32[]{:T(128)}, f32[256,256]{0,1:T(8,128)S(1)}, s32[2,2]{1,0:T(2,128)S(1)}, f32[2,128,128]{2,1,0:T(8,128)S(1)}, s32[]{:T(128)}) while((s32[]{:T(128)}, f32[256,256]{0,1:T(8,128)S(1)}, s32[2,2]{1,0:T(2,128)S(1)}, f32[2,128,128]{2,1,0:T(8,128)S(1)}, s32[]{:T(128)}) %tuple.30), condition=%wide.while_cond, body=%wide.while_body.sunk | while | flops 2 | bytes 393321 | solution.py:45
  82.4 0.6 fusion.34
  83.0 1.4 dynamic-slice.13
  84.3 0.1 copy.25
  84.5 0.6 fusion.34
  85.1 1.4 dynamic-slice.13
  86.5 0.1 copy.25
  86.6 19.9 %custom-call.16 = f32[2,128,128]{1,2,0:T(8,128)S(1)} custom-call(f32[2,128,128]{2,1,0:T(8,128)S(1)} %get-tuple-element.10), custom_call_target="InvertDiagBlocksLowerTriangular" | custom-call | tf_op jit(solution)/shard_map/jit(_solve_triangular)/triangular_solve | solution.py:45
  106.5 0.1 dynamic_slice.9
  106.6 0.7 copy.21
  107.3 0.3 fusion.6
  107.5 0.3 convolution_subtract_fusion
  107.8 0.3 fusion.9
  108.2 3.5 %fusion = f32[256,2048]{1,0:T(8,128)S(1)} fusion(f32[2048,256]{0,1:T(8,128)} %all-gather.3.cloned.1.call-done, f32[128,256]{1,0:T(8,128)S(1)} %fusion.9, f32[128,256]{1,0:T(8,128)S(1)} %fusion.6), kind=kOutput, calls=%fused_computation.5 | convolution fusion | flops 1610678272 | bytes 4456448 | tf_op jit(solution)/shard_map/dot_general | solution.py:48
  111.7 0.1 copy.23
  111.8 0.7 select_bitcast_fusion
  112.6 0.8 dynamic-slice_bitcast_fusion
  113.4 55.0 %all-reduce.3.cloned.1.call-done = f32[256,256]{1,0:T(8,128)} async-done(((f32[256,256]{1,0:T(8,128)}), f32[256,256]{1,0:T(8,128)}) %all-reduce.3.cloned.1.call-update) | async-done | bytes 262160 | tf_op jit(solution)/shard_map/psum | solution.py:9
  168.4 6.1 %subtract_select_fusion = f32[2048,256]{1,0:T(8,128)} fusion(f32[2048,256]{1,0:T(8,128)} %param.5, f32[256,2048]{1,0:T(8,128)S(1)} %fusion, f32[256,256]{1,0:T(8,128)} %all-reduce.3.cloned.1.call-done, s32[256]{0:T(256)S(1)} %iota_add_fusion, s32[2048]{0:T(1024)S(1)} %fusion.22), kind=kOutput, calls=%fused_computation.2 | convolution fusion | flops 1612185600 | bytes 6562816 | tf_op jit(solution)/shard_map/dot_general | solution.py:62
  (30 shorter events, 0.5 us)
Async XLA Ops:
  7.2 101.0 %all-gather.3.cloned.1.call-start = ((), (), s32[]{:S(2)}) async-start(), calls=%async_computation | async-start | bytes 2621440 | tf_op jit(solution)/shard_map/all_gather | solution.py:44
  17.2 6.3 %collective-permute-start = (f32[32,256]{0,1:T(8,128)S(1)}, f32[32,256]{0,1:T(8,128)S(1)}, u32[]{:S(2)}, u32[]{:S(2)}) collective-permute-start(f32[32,256]{0,1:T(8,128)S(1)} %bitcast.42), channel_id=1, source_target_pairs={{0,4},{4,8},{8,12},{12,16},{16,20},{20,24},{24,28},{28,0},{1,5},{5... | collective-permute-start | bytes 98312 | tf_op jit(solution)/shard_map/ppermute | solution.py:28
  17.3 6.3 %collective-permute-start.1 = (f32[32,256]{0,1:T(8,128)S(1)}, f32[32,256]{0,1:T(8,128)S(1)}, u32[]{:S(2)}, u32[]{:S(2)}) collective-permute-start(f32[32,256]{0,1:T(8,128)S(1)} %bitcast.43), channel_id=1, source_target_pairs={{0,28},{4,0},{8,4},{12,8},{16,12},{20,16},{24,20},{28,24},{1,29},{... | collective-permute-start | bytes 98312 | tf_op jit(solution)/shard_map/ppermute | solution.py:33
  20.8 147.6 %all-reduce.3.cloned.1.call-start = ((), (), s32[]{:S(2)}) async-start(), calls=%async_computation.1 | async-start | bytes 524288 | tf_op jit(solution)/shard_map/psum | solution.py:9
  23.5 7.3 %collective-permute-start.2 = (f32[32,256]{0,1:T(8,128)S(1)}, f32[32,256]{0,1:T(8,128)S(1)}, u32[]{:S(2)}, u32[]{:S(2)}) collective-permute-start(f32[32,256]{0,1:T(8,128)S(1)} %collective-permute-done), channel_id=1, source_target_pairs={{0,4},{4,8},{8,12},{12,16},{16,20},{20,24},{24,28},{28,0},{1,5},{5... | collective-permute-start | bytes 98312 | tf_op jit(solution)/shard_map/ppermute | solution.py:28
  23.6 7.4 %collective-permute-start.3 = (f32[32,256]{0,1:T(8,128)S(1)}, f32[32,256]{0,1:T(8,128)S(1)}, u32[]{:S(2)}, u32[]{:S(2)}) collective-permute-start(f32[32,256]{0,1:T(8,128)S(1)} %collective-permute-done.1), channel_id=1, source_target_pairs={{0,28},{4,0},{8,4},{12,8},{16,12},{20,16},{24,20},{28,24},{1,29},{... | collective-permute-start | bytes 98312 | tf_op jit(solution)/shard_map/ppermute | solution.py:33
  30.9 6.4 %collective-permute-start.4 = (f32[32,256]{0,1:T(8,128)S(1)}, f32[32,256]{0,1:T(8,128)S(1)}, u32[]{:S(2)}, u32[]{:S(2)}) collective-permute-start(f32[32,256]{0,1:T(8,128)S(1)} %collective-permute-done.2), channel_id=1, source_target_pairs={{0,4},{4,8},{8,12},{12,16},{16,20},{20,24},{24,28},{28,0},{1,5},{5... | collective-permute-start | bytes 98312 | tf_op jit(solution)/shard_map/ppermute | solution.py:28
  30.9 12.8 %collective-permute-start.5 = (f32[32,256]{0,1:T(8,128)S(1)}, f32[32,256]{0,1:T(8,128)S(1)}, u32[]{:S(2)}, u32[]{:S(2)}) collective-permute-start(f32[32,256]{0,1:T(8,128)S(1)} %collective-permute-done.3), channel_id=1, source_target_pairs={{0,28},{4,0},{8,4},{12,8},{16,12},{20,16},{24,20},{28,24},{1,29},{... | collective-permute-start | bytes 98312 | tf_op jit(solution)/shard_map/ppermute | solution.py:33
  37.2 7.9 %collective-permute-start.6 = (f32[32,256]{0,1:T(8,128)S(1)}, f32[32,256]{0,1:T(8,128)S(1)}, u32[]{:S(2)}, u32[]{:S(2)}) collective-permute-start(f32[32,256]{0,1:T(8,128)S(1)} %collective-permute-done.4), channel_id=1, source_target_pairs={{0,4},{4,8},{8,12},{12,16},{16,20},{20,24},{24,28},{28,0},{1,5},{5... | collective-permute-start | bytes 98312 | tf_op jit(solution)/shard_map/ppermute | solution.py:28
Sparse Core Ops, SparseCore 0:
  20.9 33.6 all-gather.2
  112.7 55.6 all-reduce.2
